TPU v7x, 128 devices: a whole 4x4x4 slice. The times are simulated.
128 devices in a mesh: seq: 16 (over z, y_lo, core), head: 8 (over x, y_hi).
Axes of the slice: x: 4, y: 4 (y_hi: 2, y_lo: 2; y = y_hi * 2 + y_lo), z: 4, core: 2. Of those that a mesh axis runs over, the one named last changes fastest.
Arguments:
- tokens: bfloat16 [128, 512, 1024], P('seq'), may hold values from -36 to 36
- lengths: int32 [128], P('seq'), may hold values from 1 to 512, 32768 in all
- attn_in: float32 [1024, 3, 1024], P(('seq', 'head')), may hold values from -0.4 to 0.4
- attn_out: float32 [1024, 1024], P(None, ('seq', 'head')), may hold values from -0.1875 to 0.1875
- mlp_in: float32 [1024, 4096], P(('seq', 'head')), may hold values from -0.1875 to 0.1875
- mlp_out: float32 [4096, 1024], P(None, ('seq', 'head')), may hold values from -0.09375 to 0.09375
- norm_gain: float32 [2, 1024], replicated, may hold values from 0.5 to 1.5
- norm_shift: float32 [2, 1024], replicated, may hold values from -3 to 3
Outputs:
- encoded: bfloat16 [128, 512, 1024], P('seq', 'head')
- key_cache: bfloat16 [128, 512, 1024], P('seq', None, 'head')
- value_cache: bfloat16 [128, 512, 1024], P('seq', None, 'head')
Inputs may be any that keep to these rules, and one draw needn't show every extreme that they name: `lengths`: some prompt has exactly 512 tokens.
All inputs are finite; a program needn't handle non-finite values. No bound on the sum of `lengths` on one device may be relied on, other than what follows from the above.
Results may differ from a plain program's by a relative error of at most 0.02.
Values may be sent and summed in bfloat16 or wider, within the bound.
A program may use at most 128 MiB of HBM per device.

v0:
```python
import math
import jax
import jax.numpy as jnp
from jax import lax
from jax.sharding import PartitionSpec as P

DH = 64
EPSILON = 1e-05


def layer_norm(values, gain, shift):
    center = values - jnp.mean(values, axis=-1, keepdims=True)
    spread = jnp.mean(center * center, axis=-1, keepdims=True)
    return center * lax.rsqrt(spread + EPSILON) * gain + shift


def regroup_weights(attn_in, attn_out, mlp_in, mlp_out, heads_axis):
    rows = attn_in.shape[0]
    model_width = attn_in.shape[2]
    hidden_width = mlp_in.shape[1]
    block_width = model_width // heads_axis
    hidden_block = hidden_width // heads_axis
    in_piece = attn_in.astype(jnp.bfloat16).reshape(rows, 3, heads_axis, block_width)
    in_piece = jnp.transpose(in_piece, (0, 2, 1, 3)).reshape(rows, heads_axis, 3 * block_width)
    up_piece = mlp_in.astype(jnp.bfloat16).reshape(rows, heads_axis, hidden_block)
    out_piece = attn_out.astype(jnp.bfloat16).T.reshape(rows, heads_axis, block_width)
    down_piece = mlp_out.astype(jnp.bfloat16).T.reshape(rows, heads_axis, hidden_block)
    packed = jnp.concatenate([in_piece, up_piece, out_piece, down_piece], axis=2)
    packed = lax.all_to_all(packed, "head", 1, 0, tiled=True)
    packed = packed.reshape(rows * heads_axis, packed.shape[2])
    whole = lax.all_gather(packed, "seq", axis=0, tiled=True)
    edges = [
        0,
        3 * block_width,
        3 * block_width + hidden_block,
        4 * block_width + hidden_block,
        4 * block_width + 2 * hidden_block,
    ]
    qkv_weight = whole[:, edges[0] : edges[1]].reshape(-1, 3, block_width)
    up_weight = whole[:, edges[1] : edges[2]]
    proj_weight_t = whole[:, edges[2] : edges[3]]
    down_weight_t = whole[:, edges[3] : edges[4]]
    return (qkv_weight, up_weight, proj_weight_t, down_weight_t)


def shards(tokens, lengths, attn_in, attn_out, mlp_in, mlp_out, norm_gain, norm_shift):
    heads_axis = lax.axis_size("head")
    head_index = lax.axis_index("head")
    prompts = tokens.shape[0]
    seq_len = tokens.shape[1]
    model_width = tokens.shape[2]
    block_width = model_width // heads_axis
    local_heads = block_width // DH
    qkv_weight, up_weight, proj_weight_t, down_weight_t = regroup_weights(
        attn_in, attn_out, mlp_in, mlp_out, heads_axis
    )
    projected = jnp.einsum(
        "pld,dte->plte", tokens, qkv_weight, preferred_element_type=jnp.float32
    ).astype(jnp.bfloat16)
    positions = jnp.arange(seq_len, dtype=jnp.int32)
    inside = positions[None, :] < lengths[:, None]
    key_part = projected[:, :, 1]
    value_part = projected[:, :, 2]
    queries = projected[:, :, 0].reshape(prompts, seq_len, local_heads, DH)
    key_heads = key_part.reshape(prompts, seq_len, local_heads, DH)
    value_heads = value_part.reshape(prompts, seq_len, local_heads, DH)
    scores = jnp.einsum(
        "pqhd,pkhd->phqk", queries, key_heads, preferred_element_type=jnp.float32
    ) * (1.0 / math.sqrt(DH))
    scores = jnp.where(inside[:, None, None, :], scores, -1e30)
    row_peak = jnp.max(scores, axis=-1, keepdims=True)
    raised = jnp.exp(scores - row_peak)
    weights = (raised / jnp.sum(raised, axis=-1, keepdims=True)).astype(jnp.bfloat16)
    context = jnp.einsum(
        "phqk,pkhd->pqhd", weights, value_heads, preferred_element_type=jnp.float32
    )
    context = context.astype(jnp.bfloat16).reshape(prompts, seq_len, block_width)
    key_cache = jnp.where(inside[:, :, None], key_part, jnp.zeros_like(key_part))
    value_cache = jnp.where(inside[:, :, None], value_part, jnp.zeros_like(value_part))
    row_count = seq_len // heads_axis
    row_start = head_index * row_count
    attn_partial = jnp.einsum(
        "pld,ed->ple", context, proj_weight_t, preferred_element_type=jnp.float32
    )
    attn_total = lax.psum(attn_partial.astype(jnp.bfloat16), "head").astype(jnp.float32)
    normed = layer_norm(
        tokens.astype(jnp.float32) + attn_total, norm_gain[0], norm_shift[0]
    ).astype(jnp.bfloat16)
    hidden = jax.nn.gelu(
        jnp.einsum("pld,df->plf", normed, up_weight, preferred_element_type=jnp.float32),
        approximate=False,
    ).astype(jnp.bfloat16)
    mlp_partial = jnp.einsum(
        "plf,ef->ple", hidden, down_weight_t, preferred_element_type=jnp.float32
    )
    mlp_rows = lax.psum_scatter(
        mlp_partial.astype(jnp.bfloat16), "head", scatter_dimension=1, tiled=True
    ).astype(jnp.float32)
    normed_rows = lax.dynamic_slice_in_dim(normed, row_start, row_count, 1)
    finished = layer_norm(normed_rows.astype(jnp.float32) + mlp_rows, norm_gain[1], norm_shift[1])
    inside_rows = lax.dynamic_slice_in_dim(inside, row_start, row_count, 1)
    encoded = jnp.where(inside_rows[:, :, None], finished, 0.0).astype(jnp.bfloat16)
    return (encoded, key_cache, value_cache)


def solution(mesh):
    in_specs = (
        P("seq", None, None),
        P("seq"),
        P(("seq", "head"), None, None),
        P(None, ("seq", "head")),
        P(("seq", "head"), None),
        P(None, ("seq", "head")),
        P(),
        P(),
    )
    out_specs = (P("seq", "head", None), P("seq", None, "head"), P("seq", None, "head"))
    return jax.shard_map(shards, mesh=mesh, in_specs=in_specs, out_specs=out_specs, check_vma=False)
```

profile of v0, /device:TPU:1, one launch (start us, length us, event | category | flops | bytes accessed | tf_op | source)
XLA Modules:
  0.0 626.0 jit_solution(456908509169203489)
XLA Ops:
  7.2 0.0 all-gather.2.cloned.1.call-start
  7.2 0.8 convert_bitcast_fusion.2
  8.0 0.9 copy_bitcast_fusion
  8.9 0.9 convert_element_type.56
  9.8 0.9 convert_element_type.58
  10.7 14.5 %all_to_all.15 = bf16[8,8,1536]{2,0,1:T(8,128)(2,1)} all-to-all(bf16[8,8,1536]{2,0,1:T(8,128)(2,1)S(1)} %pad_maximum_fusion), channel_id=1, replica_groups=mesh['seq'=16,'head'=8] {'head'}, dimensions={1} | all-to-all | bytes 393216 | tf_op jit(solution)/shard_map/all_to_all | solution.py:29
  25.2 0.0 all-reduce.2.cloned.1.call-start
  25.3 0.7 iota_compare_fusion
  26.0 35.7 %all-gather.2.cloned.1.call-done = bf16[1024,1536]{1,0:T(8,128)(2,1)} async-done(((bf16[64,1536]{1,0:T(8,128)(2,1)}), bf16[1024,1536]{1,0:T(8,128)(2,1)}) %all-gather.2.cloned.1.call-update) | async-done | bytes 3145744 | tf_op jit(solution)/shard_map/all_gather | solution.py:31
  61.7 1.2 slice.44
  62.9 1.2 copy.12
  64.0 7.1 %convert_bitcast_fusion = bf16[8,512,3,128]{1,3,0,2:T(8,128)(2,1)S(1)} fusion(bf16[1024,3,128,1]{0,2,3,1:T(8,128)(2,1)} %bitcast.69, bf16[8,512,1024]{2,1,0:T(8,128)(2,1)} %param.8), kind=kOutput, calls=%fused_computation.71 | convolution fusion | flops 3222798336 | bytes 12320768 | tf_op jit(solution)/shard_map/pld,dte->plte/dot_general | solution.py:57
  71.1 1.8 fusion.96
  72.9 10.7 %fusion.99 = (f32[8,2,512]{2,1,0:T(2,128)S(1)}, f32[8,2,512,512]{2,3,1,0:T(8,128)}) fusion(pred[8,512]{1,0:T(8,128)(4,1)S(1)} %iota_compare_fusion, bf16[8,512,2,64]{1,3,2,0:T(8,128)(2,1)} %bitcast.68, bf16[8,512,2,64]{1,3,2,0:T(8,128)(2,1)} %bitcast.67), kind=kOutput, calls=%fused_computation.135 | convolution fusion | flops 553648640 | bytes 18911232 | tf_op jit(solution)/shard_map/sub | solution.py:72
  83.7 7.7 %fusion.59 = bf16[8,2,64,512]{3,2,1,0:T(8,128)(2,1)S(1)} fusion(bf16[8,512,2,64]{1,3,2,0:T(8,128)(2,1)} %bitcast.66, f32[8,2,512,512]{2,3,1,0:T(8,128)} %get-tuple-element.18, f32[8,2,512]{2,1,0:T(2,128)S(1)} %get-tuple-element.17), kind=kOutput, calls=%fused_computation.80 | convolution fusion | flops 545783808 | bytes 18907136 | tf_op jit(solution)/shard_map/phqk,pkhd->pqhd/dot_general | solution.py:74
  91.4 6.5 %convolution_convert_fusion = bf16[8,512,1024]{2,1,0:T(8,128)(2,1)} fusion(bf16[8,512,128]{1,2,0:T(8,128)(2,1)S(1)} %bitcast.65, bf16[1024,1536]{1,0:T(8,128)(2,1)} %all-gather.2.cloned.1.call-done), kind=kOutput, calls=%fused_computation.38 | convolution fusion | flops 1077936128 | bytes 9699328 | tf_op jit(solution)/shard_map/pld,ed->ple/dot_general | solution.py:82
  97.9 0.2 reduce-scatter.2.cloned.1.call-start
  98.2 341.3 %all-reduce.2.cloned.1.call-done = bf16[8,512,1024]{2,1,0:T(8,128)(2,1)} async-done(((bf16[8,512,1024]{2,1,0:T(8,128)(2,1)}), bf16[8,512,1024]{2,1,0:T(8,128)(2,1)}) %all-reduce.2.cloned.1.call-update) | async-done | bytes 8388624 | tf_op jit(solution)/shard_map/psum | solution.py:85
  439.5 8.0 %fusion.2 = f32[8,512]{1,0:T(8,128)S(1)} fusion(bf16[8,512,1024]{2,1,0:T(8,128)(2,1)} %all-reduce.2.cloned.1.call-done, bf16[8,512,1024]{2,1,0:T(8,128)(2,1)} %param.8), kind=kLoop, calls=%fused_computation.8 | loop fusion | flops 16773120 | bytes 16793600 | tf_op jit(solution)/shard_map/reduce_sum | solution.py:12
  447.6 8.0 %multiply_reduce_fusion = f32[8,512]{1,0:T(8,128)S(1)} fusion(bf16[8,512,1024]{2,1,0:T(8,128)(2,1)} %all-reduce.2.cloned.1.call-done, bf16[8,512,1024]{2,1,0:T(8,128)(2,1)} %param.8, f32[8,512]{1,0:T(8,128)S(1)} %broadcast_multiply_fusion), kind=kLoop, calls=%fused_computation.2 | loop fusion | flops 25161728 | bytes 16809984 | tf_op jit(solution)/shard_map/reduce_sum | solution.py:13
  455.6 0.2 copy-done
  455.9 6.7 %add_convert_fusion = bf16[8,512,1024]{2,1,0:T(8,128)(2,1)S(1)} fusion(bf16[8,512,1024]{2,1,0:T(8,128)(2,1)S(1)} %copy-done, bf16[8,512,1024]{2,1,0:T(8,128)(2,1)} %param.8, f32[1024]{0:T(1024)S(1)} %bitcast.76, f32[1024]{0:T(1024)S(1)} %bitcast.75, f32[8,512]{1,0:T(8,128)S(1)} %add_rsqrt_fusion, f32[8,512]{1,0:T(8,128)S(1)} %broadcast_multiply_fusion), kind=kLoop, calls=%fused_computation.1 | loop fusion | flops 33554432 | bytes 25206784 | tf_op jit(solution)/shard_map/convert_element_type | solution.py:88
  462.6 6.8 %fusion.54 = (u8[512,512]{1,0:T(8,128)(4,1)S(1)}, u8[512,512]{1,0:T(8,128)(4,1)S(1)}, f32[8,512,512]{2,1,0:T(8,128)S(1)}) fusion(bf16[8,512,1024]{2,1,0:T(8,128)(2,1)S(1)} %add_convert_fusion, bf16[1024,1536]{1,0:T(8,128)(2,1)S(1)} %copy-done.2), kind=kOutput, calls=%fused_computation.76 | convolution fusion | flops 4321705984 | bytes 18350080 | tf_op jit(solution)/shard_map/pld,df->plf/dot_general | solution.py:90
  469.4 23.6 %convolution_convert_fusion.1 = bf16[8,512,1024]{2,1,0:T(8,128)(2,1)} fusion(f32[8,512,512]{2,1,0:T(8,128)S(1)} %get-tuple-element.19, u8[512,512]{1,0:T(8,128)(4,1)S(1)} %get-tuple-element.7, u8[512,512]{1,0:T(8,128)(4,1)S(1)} %get-tuple-element.6, bf16[1024,1536]{1,0:T(8,128)(2,1)S(1)} %copy-done.2), kind=kOutput, calls=%fused_computation.39 | convolution fusion | flops 4445962240 | bytes 18350080 | tf_op jit(solution)/shard_map/plf,ef->ple/dot_general | solution.py:93
  493.0 0.1 constant_dynamic-slice_fusion
  493.1 1.5 bitcast_select_fusion
  494.6 2.3 copy.16
  496.8 2.3 copy.15
  499.1 113.2 %reduce-scatter.2.cloned.1.call-done = bf16[8,64,1024]{2,1,0:T(8,128)(2,1)} async-done(((bf16[8,512,1024]{2,1,0:T(8,128)(2,1)}), bf16[8,64,1024]{2,1,0:T(8,128)(2,1)}) %reduce-scatter.2.cloned.1.call-update) | async-done | bytes 1048592 | tf_op jit(solution)/shard_map/reduce_scatter | solution.py:96
  612.2 1.9 fusion.56
  614.1 2.0 multiply_reduce_fusion.1
  616.2 3.2 select_convert_fusion
  (19 shorter events, 0.1 us)
Async XLA Ops:
  7.2 54.5 %all-gather.2.cloned.1.call-start = ((), (), s32[]{:S(2)}) async-start(), calls=%async_computation.2 | async-start | bytes 3342336 | tf_op jit(solution)/shard_map/all_gather | solution.py:31
  25.2 414.3 %all-reduce.2.cloned.1.call-start = ((), (), s32[]{:S(2)}) async-start(), calls=%async_computation.3 | async-start | bytes 16777216 | tf_op jit(solution)/shard_map/psum | solution.py:85
  91.4 6.8 %copy-start.3 = (f32[2,1024]{1,0:T(2,128)S(1)}, f32[2,1024]{1,0:T(2,128)}, u32[]{:S(2)}) copy-start(f32[2,1024]{1,0:T(2,128)} %param.14) | copy-start | bytes 24580
  91.4 6.8 %copy-start.4 = (f32[2,1024]{1,0:T(2,128)S(1)}, f32[2,1024]{1,0:T(2,128)}, u32[]{:S(2)}) copy-start(f32[2,1024]{1,0:T(2,128)} %param.15) | copy-start | bytes 24580
  97.9 514.3 %reduce-scatter.2.cloned.1.call-start = ((), (), s32[]{:S(2)}) async-start(), calls=%async_computation.4 | async-start | bytes 9437184 | tf_op jit(solution)/shard_map/reduce_scatter | solution.py:96
  447.6 8.3 %copy-start = (bf16[8,512,1024]{2,1,0:T(8,128)(2,1)S(1)}, bf16[8,512,1024]{2,1,0:T(8,128)(2,1)}, u32[]{:S(2)}) copy-start(bf16[8,512,1024]{2,1,0:T(8,128)(2,1)} %all-reduce.2.cloned.1.call-done) | copy-start | bytes 25165828
  455.9 6.7 %copy-start.2 = (bf16[1024,1536]{1,0:T(8,128)(2,1)S(1)}, bf16[1024,1536]{1,0:T(8,128)(2,1)}, u32[]{:S(2)}) copy-start(bf16[1024,1536]{1,0:T(8,128)(2,1)} %all-gather.2.cloned.1.call-done) | copy-start | bytes 9437188
  462.6 6.8 %copy-start.1 = (bf16[8,512,1024]{2,1,0:T(8,128)(2,1)}, bf16[8,512,1024]{2,1,0:T(8,128)(2,1)S(1)}, u32[]{:S(2)}) copy-start(bf16[8,512,1024]{2,1,0:T(8,128)(2,1)S(1)} %add_convert_fusion) | copy-start | bytes 25165828
Sparse Core Ops, SparseCore 0:
  25.3 36.2 all-gather.1
  98.1 341.4 all-reduce.1
  493.1 119.0 reduce-scatter.1
where the time goes:
time: 627 us; the launch traced here: 626 us
  waiting for transfers between devices  490 us (78%)
  matrix products  62.5 us (10%)
  other arithmetic  35.6 us (6%)
  blocking collectives  14.5 us (2%)
  between operations  13.9 us (2%)
  local copies, waits for them, and re-layouts  9.03 us (1%)
    psum x1, waiting for transfers between devices, shards(): lax.psum(attn_partial.astype(jnp.bfloat16), 'head').astype(jnp.float32)  341 us
    reduce_scatter x1, waiting for transfers between devices, shards(): lax.psum_scatter(mlp_partial.astype(jnp.bfloat16), 'head', scatter_dimens...  113 us
    all_gather x1, waiting for transfers between devices, regroup_weights(): whole = lax.all_gather(packed, 'seq', axis=0, tiled=True)  35.7 us
    dot_general x1, matrix products, shards(): jnp.einsum('plf,ef->ple', hidden, down_weight_t, preferred_element_type=j...  23.6 us
    all_to_all x1, blocking collectives, regroup_weights(): packed = lax.all_to_all(packed, 'head', 1, 0, tiled=True)  14.5 us
  transfers between devices with their start and end apart: 3, of which 3 were waited for; matrix products, arithmetic and copies ran while one was open for 1% of the time, Pallas kernels for 0%

commit v1 on v0

--- a/solution.py
+++ b/solution.py
@@ -82,7 +82,9 @@
     attn_partial = jnp.einsum(
         "pld,ed->ple", context, proj_weight_t, preferred_element_type=jnp.float32
     )
-    attn_total = lax.psum(attn_partial.astype(jnp.bfloat16), "head").astype(jnp.float32)
+    attn_total = jnp.sum(lax.all_gather(attn_partial.astype(jnp.bfloat16), "head"), axis=0).astype(
+        jnp.float32
+    )
     normed = layer_norm(
         tokens.astype(jnp.float32) + attn_total, norm_gain[0], norm_shift[0]
     ).astype(jnp.bfloat16)

time: 627 us -> 952 us (1.52)
  waiting for transfers between devices: 490 us -> 788 us
  other arithmetic: 35.6 us -> 61.7 us
    all_gather x0 -> x1, waiting for transfers between devices: none -> 647 us  [shards(): lax.all_gather(attn_partial.astype(jnp.bfloat16), 'head')]
    psum x1 -> x0, waiting for transfers between devices: 341 us -> none  [shards(): lax.psum(attn_partial.astype(jnp.bfloat16), 'head').astype(jnp.float32)]
    reduce_sum x0 -> x1, other arithmetic: none -> 25.9 us  [shards(): jnp.sum(lax.all_gather(attn_partial.astype(jnp.bfloat16), 'head'), axis=0)]
where the time goes in v1:
time: 952 us; the launch traced here: 951 us
  waiting for transfers between devices  788 us (83%)
  matrix products  62.5 us (7%)
  other arithmetic  61.7 us (6%)
  blocking collectives  14.5 us (2%)
  between operations  13.9 us (1%)
  local copies, waits for them, and re-layouts  10.1 us (1%)
    all_gather x1, waiting for transfers between devices, shards(): lax.all_gather(attn_partial.astype(jnp.bfloat16), 'head')  647 us
    reduce_scatter x1, waiting for transfers between devices, shards(): lax.psum_scatter(mlp_partial.astype(jnp.bfloat16), 'head', scatter_dimens...  105 us
    all_gather x1, waiting for transfers between devices, regroup_weights(): whole = lax.all_gather(packed, 'seq', axis=0, tiled=True)  35.7 us
    reduce_sum x1, other arithmetic, shards(): jnp.sum(lax.all_gather(attn_partial.astype(jnp.bfloat16), 'head'), axis=0)  25.9 us
    dot_general x1, matrix products, shards(): jnp.einsum('plf,ef->ple', hidden, down_weight_t, preferred_element_type=j...  23.6 us
  transfers between devices with their start and end apart: 3, of which 3 were waited for; matrix products, arithmetic and copies ran while one was open for 1% of the time, Pallas kernels for 0%

profile of v1, /device:TPU:1, one launch (start us, length us, event | category | flops | bytes accessed | tf_op | source)
XLA Modules:
  0.0 951.0 jit_solution(5350559928532493507)
XLA Ops:
  7.2 0.8 convert_bitcast_fusion.2
  8.0 0.9 copy_bitcast_fusion
  8.9 0.9 convert_element_type.58
  9.8 0.9 convert_element_type.60
  10.7 14.5 %all_to_all.15 = bf16[8,8,1536]{2,0,1:T(8,128)(2,1)} all-to-all(bf16[8,8,1536]{2,0,1:T(8,128)(2,1)S(1)} %pad_maximum_fusion), channel_id=1, replica_groups=mesh['seq'=16,'head'=8] {'head'}, dimensions={1} | all-to-all | bytes 393216 | tf_op jit(solution)/shard_map/all_to_all | solution.py:29
  25.3 0.7 iota_compare_fusion
  26.0 35.7 %all-gather.4.cloned.1.call-done = bf16[1024,1536]{1,0:T(8,128)(2,1)} async-done(((bf16[64,1536]{1,0:T(8,128)(2,1)}), bf16[1024,1536]{1,0:T(8,128)(2,1)}) %all-gather.4.cloned.1.call-update) | async-done | bytes 3145744 | tf_op jit(solution)/shard_map/all_gather | solution.py:31
  61.7 1.2 slice.44
  62.9 0.3 copy.18
  63.2 9.2 convert_bitcast_fusion
  72.4 1.7 copy-done.2
  74.0 0.3 fusion.96
  74.4 8.9 fusion.99
  83.3 7.4 fusion.59
  90.7 6.5 convolution_convert_fusion
  97.2 0.2 reduce-scatter.2.cloned.1.call-start
  97.5 647.3 %all-gather.6.cloned.1.call-done = bf16[64,512,1024]{2,1,0:T(8,128)(2,1)} async-done(((bf16[8,512,1024]{2,1,0:T(8,128)(2,1)}), bf16[64,512,1024]{2,1,0:T(8,128)(2,1)}) %all-gather.6.cloned.1.call-update) | async-done | bytes 67108880 | tf_op jit(solution)/shard_map/all_gather | solution.py:85
  744.8 25.9 %reduce_sum.58 = bf16[8,512,1024]{2,1,0:T(8,128)(2,1)} reduce(bf16[8,8,512,1024]{3,2,1,0:T(8,128)(2,1)} %bitcast.22, bf16[]{:T(256)} %constant.10.clone.1), dimensions={0}, to_apply=%region_2.3 | reduce | flops 29360128 | bytes 75497472 | tf_op jit(solution)/shard_map/reduce_sum | solution.py:85
  770.7 8.0 fusion.2
  778.7 8.0 multiply_reduce_fusion
  786.7 0.2 copy-done
  787.0 6.9 add_convert_fusion
  794.0 6.8 fusion.54
  800.8 23.6 %convolution_convert_fusion.1 = bf16[8,512,1024]{2,1,0:T(8,128)(2,1)} fusion(f32[8,512,512]{2,1,0:T(8,128)S(1)} %get-tuple-element.22, u8[512,512]{1,0:T(8,128)(4,1)S(1)} %get-tuple-element.10, u8[512,512]{1,0:T(8,128)(4,1)S(1)} %get-tuple-element.9, bf16[1024,1536]{1,0:T(8,128)(2,1)S(1)} %copy-done.4), kind=kOutput, calls=%fused_computation.39 | convolution fusion | flops 4445962240 | bytes 18350080 | tf_op jit(solution)/shard_map/plf,ef->ple/dot_general | solution.py:95
  824.5 1.8 copy-done.3
  826.3 1.5 bitcast_select_fusion
  827.8 2.3 copy.22
  830.0 2.3 copy.21
  832.3 105.0 %reduce-scatter.2.cloned.1.call-done = bf16[8,64,1024]{2,1,0:T(8,128)(2,1)} async-done(((bf16[8,512,1024]{2,1,0:T(8,128)(2,1)}), bf16[8,64,1024]{2,1,0:T(8,128)(2,1)}) %reduce-scatter.2.cloned.1.call-update) | async-done | bytes 1048592 | tf_op jit(solution)/shard_map/reduce_scatter | solution.py:98
  937.3 1.9 fusion.56
  939.2 2.0 multiply_reduce_fusion.1
  941.3 3.2 select_convert_fusion
  (24 shorter events, 0.3 us)
Async XLA Ops:
  7.2 54.5 %all-gather.4.cloned.1.call-start = ((), (), s32[]{:S(2)}) async-start(), calls=%async_computation.2 | async-start | bytes 3342336 | tf_op jit(solution)/shard_map/all_gather | solution.py:31
  25.2 719.6 %all-gather.6.cloned.1.call-start = ((), (), s32[]{:S(2)}) async-start(), calls=%async_computation.4 | async-start | bytes 75497472 | tf_op jit(solution)/shard_map/all_gather | solution.py:85
  72.4 1.7 copy-start.2
  90.7 6.8 copy-start.5
  90.7 6.8 copy-start.6
  97.2 840.1 %reduce-scatter.2.cloned.1.call-start = ((), (), s32[]{:S(2)}) async-start(), calls=%async_computation.3 | async-start | bytes 9437184 | tf_op jit(solution)/shard_map/reduce_scatter | solution.py:98
  778.7 8.3 copy-start
  787.0 7.0 copy-start.4
  793.9 6.8 copy-start.1
  824.4 1.9 copy-start.3
Sparse Core Ops, SparseCore 0:
  25.3 36.2 all-gather.3
  97.4 647.3 all-gather.5
  824.6 112.7 reduce-scatter.1
